TPU v7x, 256 devices: a whole 4x4x8 slice. The times are simulated.
256 devices in a mesh: req: 32 (over z, y), tp: 8 (over x, core).
Axes of the slice: x: 4, y: 4, z: 8, core: 2. Of those that a mesh axis runs over, the one named last changes fastest.
Arguments:
- attn_heads: bfloat16 [4096, 2048], P('req', 'tp'), may hold values from -6 to 6
- residual_in: bfloat16 [4096, 4096], P('req', 'tp'), may hold values from -45 to 45
- w_out: bfloat16 [2048, 4096], P('tp'), may hold values from -0.125 to 0.125
- gain_attn: float32 [4096], P('tp'), may hold values from 0.1 to 1.9
- router: bfloat16 [4096, 8], P('tp'), may hold values from -0.09375 to 0.09375
- expert_ids: int32 [4096, 2], P('req'), may hold values from 0 to 7, all different within a row; in each aligned block of 64 rows (0 to 63, 64 to 127, ...) at most 24 rows name the same one
- lengths: int32 [32, 5], P('req'), may hold values from 1 to 64, 128 in all within a row
- placement: int32 [16], replicated, may hold values from 0 to 7, as said below
- w_gate_up: bfloat16 [32, 2, 4096, 3584], P('req', None, None, 'tp'), may hold values from -1 to 1, as said below
- w_down: bfloat16 [32, 3584, 4096], P('req', 'tp'), may hold values from -1 to 1, as said below
- gain_final: float32 [4096], P('tp'), may hold values from 0.1 to 1.9
Outputs:
- residual_out: bfloat16 [4096, 4096], P('req', 'tp')
- normed_out: bfloat16 [4096, 4096], P('req', 'tp')
Inputs may be any that keep to these rules, and one draw needn't show every extreme that they name: `expert_ids`: in each aligned block of 64 rows no expert is named by more than 24 rows, and the two experts of a row differ. `placement`: every expert is held by exactly two pairs. `w_gate_up`: index 2 s + h holds the h-th half of the hidden units of expert placement[s]; the two pairs of one expert hold equal values. `w_down`: index 2 s + h holds the h-th half of the hidden units of expert placement[s]; the two pairs of one expert hold equal values.
All inputs are finite; a program needn't handle non-finite values.
Results may differ from a plain program's by a relative error of at most 0.014.
Values may be sent and summed in bfloat16 or wider, within the bound.
A program may use at most 128 MiB of HBM per device.

v0:
```python
import jax
import jax.numpy as jnp
from jax import lax
from jax.sharding import PartitionSpec as P

epsilon = 1e-05


def on_device(
    attn_heads,
    residual_in,
    w_out,
    gain_attn,
    router,
    expert_ids,
    lengths,
    placement,
    w_gate_up,
    w_down,
    gain_final,
):
    tok_rows = attn_heads.shape[0]
    half_rows = tok_rows // 2
    feat_width = residual_in.shape[1]
    full_width = feat_width * lax.axis_size("tp")
    devices = lax.axis_size("req")
    pair_count = devices // 2
    expert_count = devices // 4
    capacity = min(half_rows, 3 * tok_rows // (2 * expert_count))
    partial_out = jnp.dot(attn_heads, w_out, preferred_element_type=jnp.float32)
    state = residual_in.astype(jnp.float32) + lax.psum_scatter(
        partial_out.astype(jnp.bfloat16), "tp", scatter_dimension=1, tiled=True
    ).astype(jnp.float32)
    router_full = router.astype(jnp.float32)
    square_sum = lax.psum(jnp.sum(state * state, axis=1), "tp")
    inverse = lax.rsqrt(square_sum / full_width + epsilon)[:, None]
    normed = state * inverse * gain_attn
    logits = lax.psum(jnp.dot(normed, router_full, precision=lax.Precision.HIGHEST), "tp")
    normed_bf = normed.astype(jnp.bfloat16)
    expert_range = jnp.arange(expert_count, dtype=jnp.int32)
    match_table = expert_ids[:, :, None] == expert_range
    chosen = jnp.sum(match_table.astype(jnp.float32) * logits[:, None, :], axis=2)
    weights = jax.nn.sigmoid(chosen - chosen[:, ::-1])
    row_index = jnp.arange(tok_rows, dtype=jnp.int32)
    live_rows = row_index < tok_rows - lengths[0, lengths.shape[1] - 1]
    held_table = (placement[:, None] == expert_range).astype(jnp.int32)
    earlier = jnp.cumsum(held_table, axis=0) - held_table
    pair_range = jnp.arange(pair_count, dtype=jnp.int32)[:, None]
    first_pair = jnp.sum(pair_range * held_table * (earlier == 0).astype(jnp.int32), axis=0)
    second_pair = jnp.sum(pair_range * held_table * (earlier == 1).astype(jnp.int32), axis=0)
    upper_half = (row_index >= half_rows)[:, None, None]
    owner_table = jnp.where(upper_half, second_pair, first_pair)
    id_hot = match_table.astype(jnp.int32) * live_rows[:, None, None].astype(jnp.int32)
    target_pair = jnp.sum(id_hot * owner_table, axis=2)
    halves_hot = id_hot.reshape(2, tok_rows, expert_count)
    running = jnp.cumsum(halves_hot, axis=1) - halves_hot
    position = jnp.sum(running * halves_hot, axis=2).reshape(tok_rows, 2)
    slot_index = jnp.where(
        live_rows[:, None], target_pair * capacity + position, pair_count * capacity
    ).reshape(-1)
    source = lax.all_gather(normed_bf, "tp", axis=1, tiled=True)
    feature_dim = source.shape[1]
    sendable = jnp.zeros((pair_count * capacity + 1, feature_dim), jnp.bfloat16)
    sendable = sendable.at[slot_index].set(jnp.repeat(source, 2, axis=0))
    per_pair = sendable[: pair_count * capacity].reshape(pair_count, 1, capacity, feature_dim)
    outgoing = jnp.broadcast_to(per_pair, (pair_count, 2, capacity, feature_dim)).reshape(
        devices, capacity, feature_dim
    )
    gate_weights = w_gate_up[0, 0]
    up_weights = w_gate_up[0, 1]
    down_weights = w_down[0]
    arrived = lax.all_to_all(outgoing, "req", split_axis=0, concat_axis=0, tiled=True)
    source_count = arrived.shape[0]
    slot_count = arrived.shape[1]
    flat_rows = arrived.reshape(source_count * slot_count, full_width)
    gate_proj = jnp.dot(flat_rows, gate_weights, preferred_element_type=jnp.float32)
    up_proj = jnp.dot(flat_rows, up_weights, preferred_element_type=jnp.float32)
    activ = (jax.nn.silu(gate_proj) * up_proj).astype(jnp.bfloat16)
    down_part = jnp.dot(activ, down_weights, preferred_element_type=jnp.float32)
    reduced = lax.psum_scatter(
        down_part.astype(jnp.bfloat16), "tp", scatter_dimension=1, tiled=True
    ).astype(jnp.float32)
    returned = lax.all_to_all(
        reduced.reshape(source_count, slot_count, feat_width).astype(jnp.bfloat16),
        "req",
        split_axis=0,
        concat_axis=0,
        tiled=True,
    ).astype(jnp.float32)
    both_halves = (
        returned.reshape(pair_count, 2, capacity, feat_width)
        .sum(axis=1)
        .reshape(pair_count * capacity, feat_width)
    )
    padded = jnp.concatenate([both_halves, jnp.zeros((1, feat_width), jnp.float32)], axis=0)
    gathered_rows = padded[slot_index].reshape(tok_rows, 2, feat_width)
    mixture = gathered_rows[:, 0] * weights[:, 0:1] + gathered_rows[:, 1] * weights[:, 1:2]
    combined = state + mixture
    final_sum = lax.psum(jnp.sum(combined * combined, axis=1), "tp")
    final_scale = lax.rsqrt(final_sum / full_width + epsilon)[:, None]
    return (
        combined.astype(jnp.bfloat16),
        (combined * final_scale * gain_final).astype(jnp.bfloat16),
    )


def solution(mesh):
    placed = (
        P("req", "tp"),
        P("req", "tp"),
        P("tp", None),
        P("tp"),
        P("tp", None),
        P("req", None),
        P("req", None),
        P(),
        P("req", None, None, "tp"),
        P("req", "tp", None),
        P("tp"),
    )
    return jax.shard_map(
        on_device,
        mesh=mesh,
        in_specs=placed,
        out_specs=(P("req", "tp"), P("req", "tp")),
        check_vma=False,
    )
```

profile of v0, /device:TPU:1, one launch (start us, length us, event | category | flops | bytes accessed | tf_op | source)
XLA Modules:
  0.0 378.7 jit_solution(5766323094708515772)
XLA Ops:
  7.3 1.5 copy-done
  8.8 2.3 convolution_convert_fusion.1
  11.1 36.3 %reduce-scatter.3.cloned.1.call-done = bf16[128,512]{1,0:T(8,128)(2,1)} async-done(((bf16[128,4096]{1,0:T(8,128)(2,1)}), bf16[128,512]{1,0:T(8,128)(2,1)}) %reduce-scatter.3.cloned.1.call-update) | async-done | bytes 131088 | tf_op jit(solution)/shard_map/reduce_scatter | solution.py:31
  47.5 1.0 multiply_reduce_fusion.1
  48.5 14.7 %psum.21 = f32[128]{0:T(128)S(1)} all-reduce(f32[128]{0:T(128)S(1)} %multiply_reduce_fusion.1), channel_id=1, replica_groups=mesh['req'=32,'tp'=8] {'tp'}, use_global_device_ids=true, to_apply=%region_8.9 | all-reduce | flops 128 | bytes 1024 | tf_op jit(solution)/shard_map/psum | solution.py:35
  63.2 1.7 fusion.23
  65.0 0.6 slice.24
  66.8 0.2 reduce_window_sum.23
  67.9 0.2 fusion.24
  68.1 22.5 %all-gather.2.cloned.1.call-done = bf16[128,4096]{1,0:T(8,128)(2,1)} async-done(((bf16[128,512]{1,0:T(8,128)(2,1)}), bf16[128,4096]{1,0:T(8,128)(2,1)}) %all-gather.2.cloned.1.call-update) | async-done | bytes 1048592 | tf_op jit(solution)/shard_map/all_gather | solution.py:61
  90.6 4.7 %broadcast_in_dim.66 = bf16[128,2,4096]{2,1,0:T(2,128)(2,1)} broadcast(bf16[128,4096]{1,0:T(8,128)(2,1)} %all-gather.2.cloned.1.call-done), dimensions={0,2} | broadcast | bytes 3145728 | tf_op jit(solution)/shard_map/broadcast_in_dim | solution.py:64
  95.2 4.1 %reshape.163 = bf16[256,4096]{1,0:T(8,128)(2,1)} reshape(bf16[128,2,4096]{2,1,0:T(2,128)(2,1)} %broadcast_in_dim.66) | data formatting | bytes 4194304 | tf_op jit(solution)/shard_map/reshape | solution.py:64
  99.3 6.6 %scatter_custom_fusion = bf16[385,4096]{1,0:T(8,128)(2,1)} fusion(s32[256]{0:T(256)S(1)} %bitcast.58, bf16[256,4096]{1,0:T(8,128)(2,1)} %reshape.163, bf16[]{:T(256)} %constant.14.clone.1), kind=kCustom, calls=%fused_computation.11 | custom fusion | bytes 3154432 | tf_op jit(solution)/shard_map/scatter | solution.py:64
  105.9 1.9 slice-done
  107.8 0.8 broadcast_in_dim.68
  108.6 148.9 %all_to_all.10 = bf16[32,24,4096]{2,1,0:T(8,128)(2,1)S(1)} all-to-all(bf16[32,24,4096]{2,1,0:T(8,128)(2,1)S(1)} %bitcast.51), channel_id=1, replica_groups=mesh['req'=32,'tp'=8] {'req'}, dimensions={0} | all-to-all | bytes 12582912 | tf_op jit(solution)/shard_map/all_to_all | solution.py:72
  257.5 2.7 copy-done.1
  260.1 4.2 %fusion.3 = f32[768,448]{0,1:T(8,128)} fusion(bf16[768,4096]{1,0:T(8,128)(2,1)S(1)} %bitcast.53, bf16[1,2,4096,448]{2,3,1,0:T(8,128)(2,1)S(1)} %bitcast.61), kind=kOutput, calls=%fused_computation.7 | convolution fusion | flops 2818572288 | bytes 11337728 | tf_op jit(solution)/shard_map/dot_general | solution.py:76
  264.4 16.3 %convolution_convert_fusion = bf16[768,4096]{1,0:T(8,128)(2,1)} fusion(bf16[1,448,4096]{2,1,0:T(8,128)(2,1)} %param.20, bf16[768,4096]{1,0:T(8,128)(2,1)} %bitcast.54, bf16[1,2,4096,448]{2,3,1,0:T(8,128)(2,1)} %param.19, f32[768,448]{0,1:T(8,128)} %fusion.3), kind=kOutput, calls=%fused_computation.2 | convolution fusion | flops 5642354688 | bytes 21299200 | tf_op jit(solution)/shard_map/dot_general | solution.py:79
  280.7 41.7 %reduce-scatter.5.cloned.1.call-done = bf16[768,512]{1,0:T(8,128)(2,1)} async-done(((bf16[768,4096]{1,0:T(8,128)(2,1)}), bf16[768,512]{1,0:T(8,128)(2,1)}) %reduce-scatter.5.cloned.1.call-update) | async-done | bytes 786448 | tf_op jit(solution)/shard_map/reduce_scatter | solution.py:80
  322.4 9.6 %all-to-all-start.1 = ((bf16[32,24,512]{2,1,0:T(8,128)(2,1)}), bf16[32,24,512]{2,1,0:T(8,128)(2,1)S(1)}, u32[]{:S(2)}, u32[]{:S(2)}) async-start(bf16[32,24,512]{2,1,0:T(8,128)(2,1)} %bitcast.56), calls=%async_computation.3 | async-start | bytes 1572864 | tf_op jit(solution)/shard_map/all_to_all | solution.py:83
  332.0 0.6 pad_clamp_fusion
  332.6 0.3 fusion.22
  332.9 13.6 %psum.22 = f32[128,8]{0,1:T(8,128)S(1)} all-reduce(f32[128,8]{0,1:T(8,128)S(1)} %fusion.22), channel_id=1, replica_groups=mesh['req'=32,'tp'=8] {'tp'}, use_global_device_ids=true, to_apply=%region_12.13 | all-reduce | flops 1024 | bytes 8192 | tf_op jit(solution)/shard_map/psum | solution.py:38
  346.5 0.6 slice_bitcast_fusion.1
  347.1 5.8 %all-to-all-done.1 = bf16[32,24,512]{2,1,0:T(8,128)(2,1)S(1)} async-done(((bf16[32,24,512]{2,1,0:T(8,128)(2,1)}), bf16[32,24,512]{2,1,0:T(8,128)(2,1)S(1)}, u32[]{:S(2)}, u32[]{:S(2)}) %all-to-all-start.1) | async-done | bytes 786464 | tf_op jit(solution)/shard_map/all_to_all | solution.py:83
  353.1 1.1 gather_fusion
  354.2 0.3 reshape.148
  354.5 0.4 fusion.32
  355.0 1.1 multiply_reduce_fusion
  356.1 14.6 %psum.23 = f32[128]{0:T(128)S(1)} all-reduce(f32[128]{0:T(128)S(1)} %get-tuple-element.4), channel_id=1, replica_groups=mesh['req'=32,'tp'=8] {'tp'}, use_global_device_ids=true, to_apply=%region_15.16 | all-reduce | flops 128 | bytes 1024 | tf_op jit(solution)/shard_map/psum | solution.py:99
  370.7 1.4 multiply_convert_fusion
  (54 shorter events, 1.9 us)
Async XLA Ops:
  7.2 1.6 copy-start
  7.2 40.3 %copy-start.2 = (bf16[128,512]{1,0:T(8,128)(2,1)S(1)}, bf16[128,512]{1,0:T(8,128)(2,1)}, u32[]{:S(2)}) copy-start(bf16[128,512]{1,0:T(8,128)(2,1)} %param.12) | copy-start | bytes 393220
  7.2 56.0 %copy-start.5 = (f32[512]{0:T(512)S(1)}, f32[512]{0:T(512)}, u32[]{:S(2)}) copy-start(f32[512]{0:T(512)} %param.14) | copy-start | bytes 6148
  7.2 57.7 %copy-start.8 = (s32[1,5]{1,0:T(1,128)S(1)}, s32[1,5]{1,0:T(1,128)}, u32[]{:S(2)}) copy-start(s32[1,5]{1,0:T(1,128)} %param.17) | copy-start | bytes 64
  7.2 59.2 %copy-start.4 = (s32[128,2]{0,1:T(2,128)S(1)}, s32[128,2]{0,1:T(2,128)}, u32[]{:S(2)}) copy-start(s32[128,2]{0,1:T(2,128)} %param.16) | copy-start | bytes 3076
  7.2 59.8 %copy-start.6 = (s32[16]{0:T(128)S(1)}, s32[16]{0:T(128)}, u32[]{:S(2)}) copy-start(s32[16]{0:T(128)} %param.18) | copy-start | bytes 196
  7.2 40.2 %reduce-scatter.3.cloned.1.call-start = ((), (), s32[]{:S(2)}) async-start(), calls=%async_computation.4 | async-start | bytes 1179648 | tf_op jit(solution)/shard_map/reduce_scatter | solution.py:31
  11.1 79.5 %all-gather.2.cloned.1.call-start = ((), (), s32[]{:S(2)}) async-start(), calls=%async_computation.5 | async-start | bytes 1179648 | tf_op jit(solution)/shard_map/all_gather | solution.py:61
  64.9 257.5 %reduce-scatter.5.cloned.1.call-start = ((), (), s32[]{:S(2)}) async-start(), calls=%async_computation.6 | async-start | bytes 7077888 | tf_op jit(solution)/shard_map/reduce_scatter | solution.py:80
  105.9 1.9 slice-start
  107.8 152.3 %slice-start.1 = ((s8[7340032]{0:T(1024)(128)(4,1)}), s8[3145728]{0:T(1024)(128)(4,1)S(1)}, s32[]{:S(2)}) async-start(s8[7340032]{0:T(1024)(128)(4,1)} %bitcast.60), calls=%async_computation.8 | async-start | bytes 6291456
  108.6 151.6 %slice-start.2 = ((s8[7340032]{0:T(1024)(128)(4,1)}), s8[4194304]{0:T(1024)(128)(4,1)S(1)}, s32[]{:S(2)}) async-start(s8[7340032]{0:T(1024)(128)(4,1)} %bitcast.60), calls=%async_computation.9 | async-start | bytes 8388608
  257.5 2.7 copy-start.1
  280.7 51.9 %copy-start.3 = (bf16[128,512]{1,0:T(8,128)(2,1)S(1)}, bf16[128,512]{1,0:T(8,128)(2,1)}, u32[]{:S(2)}) copy-start(bf16[128,512]{1,0:T(8,128)(2,1)} %reduce-scatter.3.cloned.1.call-done) | copy-start | bytes 393220
  280.7 51.9 %copy-start.7 = (bf16[512,8]{0,1:T(8,128)(2,1)S(1)}, bf16[512,8]{0,1:T(8,128)(2,1)}, u32[]{:S(2)}) copy-start(bf16[512,8]{0,1:T(8,128)(2,1)} %param.15) | copy-start | bytes 24580
  322.4 30.5 %all-to-all-start.1 = ((bf16[32,24,512]{2,1,0:T(8,128)(2,1)}), bf16[32,24,512]{2,1,0:T(8,128)(2,1)S(1)}, u32[]{:S(2)}, u32[]{:S(2)}) async-start(bf16[32,24,512]{2,1,0:T(8,128)(2,1)} %bitcast.56), calls=%async_computation.3 | async-start | bytes 1572864 | tf_op jit(solution)/shard_map/all_to_all | solution.py:83
Sparse Core Ops, SparseCore 0:
  11.2 36.2 reduce-scatter.2
  65.0 25.4 all-gather.1
  280.8 41.5 reduce-scatter.4
where the time goes:
time: 380 us; the launch traced here: 379 us
  blocking collectives  192 us (51%)
  waiting for transfers between devices  106 us (28%)
  local copies, waits for them, and re-layouts  26.3 us (7%)
  matrix products  23.1 us (6%)
  between operations  14.6 us (4%)
  starting transfers between devices  9.69 us (3%)
  other arithmetic  6.89 us (2%)
    all_to_all x1, blocking collectives, on_device(): lax.all_to_all(outgoing, 'req', split_axis=0, concat_axis=0, tiled=True)  149 us
    reduce_scatter x1, waiting for transfers between devices, on_device(): lax.psum_scatter(down_part.astype(jnp.bfloat16), 'tp', scatter_dimension=...  41.7 us
    reduce_scatter x1, waiting for transfers between devices, on_device(): lax.psum_scatter(partial_out.astype(jnp.bfloat16), 'tp', scatter_dimensio...  36.3 us
    all_gather x1, waiting for transfers between devices, on_device(): source = lax.all_gather(normed_bf, 'tp', axis=1, tiled=True)  22.5 us
    dot_general x1, matrix products, on_device(): down_part = jnp.dot(activ, down_weights, preferred_element_type=jnp.float32)  16.3 us
    psum x1, blocking collectives, on_device(): square_sum = lax.psum(jnp.sum(state * state, axis=1), 'tp')  14.7 us
    psum x1, blocking collectives, on_device(): final_sum = lax.psum(jnp.sum(combined * combined, axis=1), 'tp')  14.6 us
    psum x1, blocking collectives, on_device(): lax.psum(jnp.dot(normed, router_full, precision=lax.Precision.HIGHEST), '...  13.6 us
  transfers between devices with their start and end apart: 4, of which 4 were waited for; matrix products, arithmetic and copies ran while one was open for 1% of the time, Pallas kernels for 0%

commit v1 on v0

v1 whole, which is shorter than its diff:
```python
import functools

import jax
import jax.numpy as jnp
from jax import lax
from jax.experimental import pallas as pl
from jax.experimental.pallas import tpu as pltpu
from jax.sharding import PartitionSpec as P

MESH = pl.DeviceIdType.MESH
EPS = 1e-05
F32 = jnp.float32
BF16 = jnp.bfloat16
NUM_SEMS = 240
NT = (((1,), (1,)), ((), ()))


def offsets(count):
    order = [0]
    for step in range(1, count // 2 + 1):
        order.append(step)
        if count - step != step:
            order.append(count - step)
    return order[:count]


def mega_kernel(
    dims,
    attn, resid, w_out, gain_a, router_t, ids_t, lengths, placement, w_gu, w_d, gain_f,
    res_out, norm_out,
    wo, wg, wu, wdo, wdp, p_s, p_r, h1_s, h1_r, f1_s, f1_r, stat_s, stat_r, outb, xs,
    act_s, act_r, h_s, h_r, f_s, f_r, qx, ret_s, ret_r, fin_s, fin_r, dt, state_ref, wcol,
    loc, ss, rs,
):
    nreq, ny, nt, rows, feat, hid, cap, groups = dims
    nz, nx = nreq // ny, nt // 2
    full = nt * feat
    half_rows = rows // 2
    pairs = nreq // 2
    ct = cap // 8
    per_group = nreq // groups
    bg = per_group * ct
    grows = bg * 8

    r = lax.axis_index("req")
    t = lax.axis_index("tp")
    z, y = r // ny, r % ny
    x, c = t // 2, t % 2
    xr, xl, xo = (x + 1) % nx, (x + nx - 1) % nx, (x + 2) % nx
    tr, tl, to = xr * 2 + c, xl * 2 + c, xo * 2 + c
    tc = x * 2 + (1 - c)

    counter = [0]
    started = []

    def remote(src, dst, req, tp):
        k = counter[0]
        counter[0] += 1
        copy = pltpu.make_async_remote_copy(
            src_ref=src, dst_ref=dst, send_sem=ss.at[k], recv_sem=rs.at[k],
            device_id=(req, tp), device_id_type=MESH,
        )
        copy.start()
        started.append(copy)
        return copy

    order = [(dz, dy) for dz in offsets(nz) for dy in offsets(ny)]
    dest = [((z + dz) % nz) * ny + (y + dy) % ny for dz, dy in order]
    source = [((z + nz - dz) % nz) * ny + (y + ny - dy) % ny for dz, dy in order]

    barrier = pltpu.get_barrier_semaphore()
    for k in range(1, nt):
        pl.semaphore_signal(barrier, inc=1, device_id=(r, (t + k) % nt), device_id_type=MESH)
    for j in range(1, nreq):
        pl.semaphore_signal(barrier, inc=1, device_id=(dest[j], t), device_id_type=MESH)

    load_wo = pltpu.make_async_copy(w_out, wo, loc.at[0])
    load_wo.start()
    load_wg = pltpu.make_async_copy(w_gu.at[0, 0], wg, loc.at[1])
    load_wu = pltpu.make_async_copy(w_gu.at[0, 1], wu, loc.at[2])
    load_wd = [
        pltpu.make_async_copy(
            w_d.at[0, :, pl.ds(pl.multiple_of((2 * i + c) * feat, feat), feat)], wdo.at[i], loc.at[3 + i]
        )
        for i in range(nx)
    ]

    e_iota = lax.broadcasted_iota(jnp.int32, (8, rows), 0)
    row_iota = lax.broadcasted_iota(jnp.int32, (8, rows), 1)
    live = row_iota < rows - lengths[0, lengths.shape[1] - 1]
    ids = [jnp.broadcast_to(ids_t[k : k + 1, :], (8, rows)) for k in range(2)]
    match = [jnp.where((e_iota == ids[k]) & live, 1.0, 0.0).astype(F32) for k in range(2)]
    hot = match[0] + match[1]
    sub = lax.broadcasted_iota(jnp.int32, (rows, rows), 0)
    lane = lax.broadcasted_iota(jnp.int32, (rows, rows), 1)
    earlier = (sub < lane) & ((sub >= half_rows) == (lane >= half_rows))
    running = jnp.dot(hot.astype(BF16), jnp.where(earlier, 1.0, 0.0).astype(BF16), preferred_element_type=F32)
    seen = jnp.zeros((8, rows), jnp.int32)
    target = jnp.zeros((8, rows), jnp.int32)
    want = jnp.where(row_iota >= half_rows, 1, 0)
    for s in range(pairs):
        held = e_iota == placement[s]
        target = jnp.where(held & (seen == want), s, target)
        seen = seen + jnp.where(held, 1, 0)
    slot = target.astype(F32) * float(cap) + running
    live1 = live[0:1, :]
    keys = [
        jnp.where(live1, jnp.sum(match[k] * slot, axis=0, keepdims=True), -1.0) for k in range(2)
    ]

    def column(vec):
        return jnp.transpose(jnp.broadcast_to(vec, (rows, rows)))

    col = lax.broadcasted_iota(jnp.int32, (8, nreq * cap), 1)
    colkey = jnp.zeros((8, nreq * cap), jnp.int32)
    for j in range(nreq):
        inside = (col >= j * cap) & (col < (j + 1) * cap)
        colkey = jnp.where(inside, (dest[j] // 2) * cap + (col - j * cap), colkey)
    colkey_f = colkey.astype(F32)
    for k in range(2):
        keyc = column(keys[k])
        for b in range(nreq * cap // 128):
            piece = jnp.broadcast_to(colkey_f[0:1, b * 128 : (b + 1) * 128], (rows, 128))
            dt[k, :, b * 128 : (b + 1) * 128] = jnp.where(keyc == piece, 1.0, 0.0).astype(BF16)

    load_wo.wait()
    load_wg.start()
    load_wu.start()
    for copy in load_wd:
        copy.start()
    heads = attn[...]
    for i in range(nx):
        w = wo[:, pl.ds(pl.multiple_of((2 * i + 1 - c) * feat, feat), feat)]
        p_s[i] = jnp.dot(heads, w, preferred_element_type=F32).astype(BF16)

    pl.semaphore_wait(barrier, nt - 1 + nreq - 1)

    p_copy = remote(p_s, p_r, r, tc)

    def own_share(i):
        w = wo[:, pl.ds(pl.multiple_of((2 * i + c) * feat, feat), feat)]
        return jnp.dot(heads, w, preferred_element_type=F32)

    own = [own_share(i) for i in (xo, xr, xl, x)]
    p_copy.wait_recv()
    share = [own[n] + p_r[i].astype(F32) for n, i in enumerate((xo, xr, xl, x))]
    h1_s[0] = share[0][:half_rows].astype(BF16)
    h1_s[1] = share[0][half_rows:].astype(BF16)
    up = remote(h1_s.at[0], h1_r.at[0], r, tr)
    down = remote(h1_s.at[1], h1_r.at[1], r, tl)
    up.wait_recv()
    f1_s[0, :half_rows] = (share[1][:half_rows] + h1_r[0].astype(F32)).astype(BF16)
    f1_s[0, half_rows:] = share[1][half_rows:].astype(BF16)
    fup = remote(f1_s.at[0], f1_r.at[0], r, tr)
    down.wait_recv()
    f1_s[1, :half_rows] = share[2][:half_rows].astype(BF16)
    f1_s[1, half_rows:] = (share[2][half_rows:] + h1_r[1].astype(F32)).astype(BF16)
    fdown = remote(f1_s.at[1], f1_r.at[1], r, tl)
    base = resid[...].astype(F32) + share[3]
    fup.wait_recv()
    fdown.wait_recv()
    state = base + f1_r[0].astype(F32) + f1_r[1].astype(F32)
    state_ref[...] = state

    wd_copies = [
        remote(w_d.at[0, :, pl.ds(pl.multiple_of((2 * i + 1 - c) * feat, feat), feat)], wdp.at[i], r, tc)
        for i in range(nx)
    ]

    ones = jnp.ones((8, feat), F32)
    gain = gain_a[...]

    def square_sums(values):
        return lax.dot_general(ones, values * values, NT, precision=lax.Precision.HIGHEST, preferred_element_type=F32)

    stat_s[0:8] = square_sums(state)
    stat_s[8:16] = lax.dot_general(
        router_t[...] * gain, state, NT, precision=lax.Precision.HIGHEST, preferred_element_type=F32
    )
    stat_copies = [remote(stat_s, stat_r.at[k - 1], r, (t + k) % nt) for k in range(1, nt)]
    total = stat_s[...]
    for k, copy in enumerate(stat_copies):
        copy.wait_recv()
        total = total + stat_r[k]
    inverse = lax.rsqrt(total[0:1] / full + EPS)
    inv_col = jnp.concatenate([column(inverse)] * (feat // rows), axis=1)
    normed = (state * inv_col * gain).astype(BF16)

    slots = lax.broadcasted_iota(jnp.int32, (pairs * cap, rows), 0)
    chosen_slot = (slots == keys[0].astype(jnp.int32)) | (slots == keys[1].astype(jnp.int32))
    scatter = jnp.where(chosen_slot, 1.0, 0.0).astype(BF16)
    sent = jnp.dot(scatter, normed, preferred_element_type=F32)
    outb[...] = sent.reshape(pairs * ct, 8, feat).astype(BF16)

    keep = pltpu.make_async_copy(
        outb.at[pl.ds((r // 2) * ct, ct)], xs.at[t, pl.ds(0, ct)], loc.at[3 + nx]
    )
    keep.start()
    a2a = [None] + [
        remote(outb.at[pl.ds((dest[j] // 2) * ct, ct)], xs.at[t, pl.ds(j * ct, ct)], dest[j], t)
        for j in range(1, nreq)
    ]

    logits = total[8:16] * inverse
    picked = [jnp.sum(match[k] * logits, axis=0, keepdims=True) for k in range(2)]
    wcol[0] = column(jax.nn.sigmoid(picked[0] - picked[1]))
    wcol[1] = column(jax.nn.sigmoid(picked[1] - picked[0]))

    load_wg.wait()
    load_wu.wait()

    gather = {}
    reduce = {}
    returns = {}

    def rows_of(g, part=0, parts=1):
        return pl.ds(g * bg + part * (bg // parts), bg // parts)

    def stage_a(g):
        for j in range(g * per_group, (g + 1) * per_group):
            if j == 0:
                keep.wait()
            else:
                a2a[j].wait_recv()
        mine = xs.at[t, rows_of(g)]
        gather[g, "right"] = remote(mine, mine, r, tr)
        gather[g, "left"] = remote(mine, mine, r, tl)
        gather[g, "own"] = remote(mine, mine, r, tc)

    def stage_b(g):
        gather[g, "right"].wait_recv()
        top = xs.at[tl, rows_of(g, 0, 2)]
        gather[g, "top"] = remote(top, top, r, tr)
        gather[g, "left"].wait_recv()
        bottom = xs.at[tr, rows_of(g, 1, 2)]
        gather[g, "bottom"] = remote(bottom, bottom, r, tl)
        for name, who in (("fwd_l", tl), ("fwd_r", tr)):
            block = xs.at[who, rows_of(g)]
            gather[g, name] = remote(block, block, r, tc)

    def stage_c(g):
        gather[g, "top"].wait_recv()
        gather[g, "bottom"].wait_recv()
        block = xs.at[to, rows_of(g)]
        gather[g, "fwd_o"] = remote(block, block, r, tc)

    def stage_m(g):
        gate = up_acc = None
        plan = (
            (t, None), (tl, None), (tr, None), (to, None),
            (tc, "own"), (xl * 2 + (1 - c), "fwd_l"), (xr * 2 + (1 - c), "fwd_r"), (xo * 2 + (1 - c), "fwd_o"),
        )
        for who, name in plan:
            if name is not None:
                gather[g, name].wait_recv()
            block = xs[who, g * bg : (g + 1) * bg].reshape(grows, feat)
            k_rows = pl.ds(pl.multiple_of(who * feat, feat), feat)
            gp = jnp.dot(block, wg[k_rows, :], preferred_element_type=F32)
            up_p = jnp.dot(block, wu[k_rows, :], preferred_element_type=F32)
            gate = gp if gate is None else gate + gp
            up_acc = up_p if up_acc is None else up_acc + up_p
        act_s[g] = (jax.nn.silu(gate) * up_acc).astype(BF16)
        reduce[g, "act"] = remote(act_s.at[g], act_r.at[g], r, tc)

    def product(g, i):
        own_part = jnp.dot(act_s[g], wdo[i], preferred_element_type=F32)
        return own_part + jnp.dot(act_r[g], wdp[i], preferred_element_type=F32)

    gh = grows // 2

    def stage_d(g):
        reduce[g, "act"].wait_recv()
        far = product(g, xo).astype(BF16)
        h_s[g, 0] = far[:gh]
        h_s[g, 1] = far[gh:]
        reduce[g, "up"] = remote(h_s.at[g, 0], h_r.at[g, 0], r, tr)
        reduce[g, "down"] = remote(h_s.at[g, 1], h_r.at[g, 1], r, tl)

    def stage_e(g):
        near = product(g, xr)
        reduce[g, "up"].wait_recv()
        f_s[g, 0, :gh] = (near[:gh] + h_r[g, 0].astype(F32)).astype(BF16)
        f_s[g, 0, gh:] = near[gh:].astype(BF16)
        reduce[g, "fup"] = remote(f_s.at[g, 0], f_r.at[g, 0], r, tr)
        near = product(g, xl)
        reduce[g, "down"].wait_recv()
        f_s[g, 1, :gh] = near[:gh].astype(BF16)
        f_s[g, 1, gh:] = (near[gh:] + h_r[g, 1].astype(F32)).astype(BF16)
        reduce[g, "fdown"] = remote(f_s.at[g, 1], f_r.at[g, 1], r, tl)
        qx[g] = product(g, x)

    def stage_f(g):
        reduce[g, "fup"].wait_recv()
        reduce[g, "fdown"].wait_recv()
        result = qx[g] + f_r[g, 0].astype(F32) + f_r[g, 1].astype(F32)
        ret_s[g * bg : (g + 1) * bg] = result.reshape(bg, 8, feat).astype(BF16)
        for j in range(g * per_group, (g + 1) * per_group):
            if j == 0:
                returns[0] = pltpu.make_async_copy(ret_s.at[pl.ds(0, ct)], ret_r.at[pl.ds(0, ct)], loc.at[4 + nx])
                returns[0].start()
            else:
                block = pl.ds(j * ct, ct)
                returns[j] = remote(ret_s.at[block], ret_r.at[block], source[j], t)

    def load_down():
        for copy in load_wd:
            copy.wait()
        for copy in wd_copies:
            copy.wait_recv()

    stage_a(0)
    stage_a(1)
    stage_b(0)
    stage_c(0)
    stage_b(1)
    stage_m(0)
    stage_a(2)
    load_down()
    stage_d(0)
    stage_c(1)
    stage_m(1)
    stage_e(0)
    stage_b(2)
    stage_a(3)
    stage_d(1)
    stage_c(2)
    stage_f(0)
    stage_m(2)
    stage_b(3)
    stage_e(1)
    stage_d(2)
    stage_c(3)
    stage_f(1)
    stage_m(3)
    stage_e(2)
    stage_d(3)
    stage_e(3)
    stage_f(2)
    stage_f(3)

    mix = [None, None]
    half = nreq // 2
    for part in range(2):
        for j in range(part * half, (part + 1) * half):
            if j == 0:
                returns[0].wait()
            else:
                returns[j].wait_recv()
        block = ret_r[part * half * ct : (part + 1) * half * ct].reshape(half * cap, feat)
        for k in range(2):
            pick = dt[k, :, part * half * cap : (part + 1) * half * cap]
            got = jnp.dot(pick, block, preferred_element_type=F32)
            mix[k] = got if mix[k] is None else mix[k] + got
    wide = [jnp.concatenate([wcol[k]] * (feat // rows), axis=1) for k in range(2)]
    combined = state_ref[...] + mix[0] * wide[0] + mix[1] * wide[1]
    res_out[...] = combined.astype(BF16)
    fin_s[...] = square_sums(combined)
    fin_copies = [remote(fin_s, fin_r.at[k - 1], r, (t + k) % nt) for k in range(1, nt)]
    total = fin_s[...]
    for k, copy in enumerate(fin_copies):
        copy.wait_recv()
        total = total + fin_r[k]
    scale = lax.rsqrt(total[0:1] / full + EPS)
    scale_col = jnp.concatenate([column(scale)] * (feat // rows), axis=1)
    norm_out[...] = (combined * scale_col * gain_f[...]).astype(BF16)
    for copy in started:
        copy.wait_send()
    assert counter[0] <= NUM_SEMS, counter[0]


def on_device(
    attn_heads, residual_in, w_out, gain_attn, router, expert_ids, lengths, placement, w_gate_up, w_down, gain_final
):
    rows = attn_heads.shape[0]
    feat = residual_in.shape[1]
    heads = attn_heads.shape[1]
    nt = lax.axis_size("tp")
    nreq = lax.axis_size("req")
    full = feat * nt
    hid = w_gate_up.shape[3]
    experts = nreq // 4
    cap = min(rows // 2, 3 * rows // (2 * experts))
    groups = 4
    ny = 4
    nx = nt // 2
    ct = cap // 8
    pairs = nreq // 2
    grows = nreq * cap // groups
    router_t = router.astype(F32).T
    if experts < 8:
        router_t = jnp.pad(router_t, ((0, 8 - experts), (0, 0)))
    vmem = pl.BlockSpec(memory_space=pltpu.VMEM)
    smem = pl.BlockSpec(memory_space=pltpu.SMEM)
    hbm = pl.BlockSpec(memory_space=pl.ANY)
    dims = (nreq, ny, nt, rows, feat, hid, cap, groups)
    out = jax.ShapeDtypeStruct((rows, feat), BF16)
    return pl.pallas_call(
        functools.partial(mega_kernel, dims),
        out_shape=(out, out),
        in_specs=[vmem, vmem, hbm, vmem, vmem, vmem, smem, smem, hbm, hbm, vmem],
        out_specs=(vmem, vmem),
        scratch_shapes=[
            pltpu.VMEM((heads, full), BF16),
            pltpu.VMEM((full, hid), BF16),
            pltpu.VMEM((full, hid), BF16),
            pltpu.VMEM((nx, hid, feat), BF16),
            pltpu.VMEM((nx, hid, feat), BF16),
            pltpu.VMEM((nx, rows, feat), BF16),
            pltpu.VMEM((nx, rows, feat), BF16),
            pltpu.VMEM((2, rows // 2, feat), BF16),
            pltpu.VMEM((2, rows // 2, feat), BF16),
            pltpu.VMEM((2, rows, feat), BF16),
            pltpu.VMEM((2, rows, feat), BF16),
            pltpu.VMEM((16, rows), F32),
            pltpu.VMEM((nt - 1, 16, rows), F32),
            pltpu.VMEM((pairs * ct, 8, feat), BF16),
            pltpu.VMEM((nt, nreq * ct, 8, feat), BF16),
            pltpu.VMEM((groups, grows, hid), BF16),
            pltpu.VMEM((groups, grows, hid), BF16),
            pltpu.VMEM((groups, 2, grows // 2, feat), BF16),
            pltpu.VMEM((groups, 2, grows // 2, feat), BF16),
            pltpu.VMEM((groups, 2, grows, feat), BF16),
            pltpu.VMEM((groups, 2, grows, feat), BF16),
            pltpu.VMEM((groups, grows, feat), F32),
            pltpu.VMEM((nreq * ct, 8, feat), BF16),
            pltpu.VMEM((nreq * ct, 8, feat), BF16),
            pltpu.VMEM((8, rows), F32),
            pltpu.VMEM((nt - 1, 8, rows), F32),
            pltpu.VMEM((2, rows, nreq * cap), BF16),
            pltpu.VMEM((rows, feat), F32),
            pltpu.VMEM((2, rows, rows), F32),
            pltpu.SemaphoreType.DMA((5 + nx,)),
            pltpu.SemaphoreType.DMA((NUM_SEMS,)),
            pltpu.SemaphoreType.DMA((NUM_SEMS,)),
        ],
        compiler_params=pltpu.CompilerParams(
            collective_id=0, has_side_effects=True, vmem_limit_bytes=60 * 1024 * 1024
        ),
    )(
        attn_heads,
        residual_in,
        w_out,
        gain_attn.reshape(1, feat),
        router_t,
        expert_ids.T,
        lengths,
        placement,
        w_gate_up,
        w_down,
        gain_final.reshape(1, feat),
    )


def solution(mesh):
    placed = (
        P("req", "tp"),
        P("req", "tp"),
        P("tp", None),
        P("tp"),
        P("tp", None),
        P("req", None),
        P("req", None),
        P(),
        P("req", None, None, "tp"),
        P("req", "tp", None),
        P("tp"),
    )
    return jax.shard_map(
        on_device,
        mesh=mesh,
        in_specs=placed,
        out_specs=(P("req", "tp"), P("req", "tp")),
        check_vma=False,
    )
```

time: 380 us -> 135 us (0.36)
  blocking collectives: 192 us -> 0 us
  Pallas kernels: 0 us -> 118 us
  waiting for transfers between devices: 106 us -> 0 us
  matrix products: 23.1 us -> 0 us
  between operations: 14.6 us -> 0.64 us
  local copies, waits for them, and re-layouts: 26.3 us -> 14.7 us
  starting transfers between devices: 9.69 us -> 0 us
  other arithmetic: 6.89 us -> 1.3 us
    all_to_all x1 -> x0, blocking collectives: 149 us -> none  [on_device(): lax.all_to_all(outgoing, 'req', split_axis=0, concat_axis=0, tiled=True)]
    pallas_call x0 -> x1, Pallas kernels: none -> 118 us  [on_device(): pl.pallas_call(functools.partial(mega_kernel, dims), out_shape=(out, out)...]
    reduce_scatter x2 -> x0, waiting for transfers between devices: 78 us -> none  [the longest x1 41.7 us: on_device(): lax.psum_scatter(down_part.astype(jnp.bfloat16), 'tp', scatter_dimension=...]
    psum x3 -> x0, blocking collectives: 42.9 us -> none  [the longest x1 14.7 us: on_device(): square_sum = lax.psum(jnp.sum(state * state, axis=1), 'tp')]
    dot_general x4 -> x0, matrix products: 23.1 us -> none  [the longest x1 16.3 us: on_device(): down_part = jnp.dot(activ, down_weights, preferred_element_type=jnp.float32)]
    all_gather x1 -> x0, waiting for transfers between devices: 22.5 us -> none  [on_device(): source = lax.all_gather(normed_bf, 'tp', axis=1, tiled=True)]
    unnamed x23 -> x3, local copies, waits for them, and re-layouts: 4.3 us -> 14.7 us
    all_to_all x1 -> x0, starting transfers between devices: 9.57 us -> none  [on_device(): lax.all_to_all(reduced.reshape(source_count, slot_count, feat_width).asty...]
  transfers between devices with their start and end apart: 4 -> 0, of which waited for: 4 -> 0; matrix products, arithmetic and copies ran while one was open for 1% -> 0% of each run, Pallas kernels for 0% -> 0%
where the time goes in v1:
time: 135 us
  Pallas kernels  118 us (87%)
  local copies, waits for them, and re-layouts  14.7 us (11%)
    pallas_call x1, Pallas kernels, on_device(): pl.pallas_call(functools.partial(mega_kernel, dims), out_shape=(out, out)...  118 us
    unnamed x3, local copies, waits for them, and re-layouts  14.7 us

profile of v1, /device:TPU:1, one launch (start us, length us, event | category | flops | bytes accessed | tf_op | source)
XLA Modules:
  0.0 134.8 jit_solution(3894032812983866072)
XLA Ops:
  0.6 1.3 convert_bitcast_fusion.router_t
  1.9 11.6 %copy.13.w_gu = bf16[1,2,4096,448]{3,2,1,0:T(8,128)(2,1)} copy(bf16[1,2,4096,448]{2,3,1,0:T(8,128)(2,1)} %param.19) | data formatting | bytes 14680064 | tf_op args[8]
  13.5 118.2 %shard_map.122 = (bf16[128,512]{1,0:T(8,128)(2,1)}, bf16[128,512]{1,0:T(8,128)(2,1)}) custom-call(bf16[128,256]{1,0:T(8,128)(2,1)} %attn.1, bf16[128,512]{1,0:T(8,128)(2,1)} %resid.1, bf16[256,4096]{1,0:T(8,128)(2,1)} %w_out.1, f32[1,512]{1,0:T(1,128)} %bitcast.5, f32[8,512]{1,0:T(8,128)} %convert_bitcast_fusion.router_t, s32[2,128]{1,0:T(2,128)} %bitcast.7, ...), custom_call_target="tpu_custom_call" | custom-call | tf_op jit(solution)/shard_map/pallas_call | solution.py:397
  131.7 1.6 %copy.16 = bf16[128,512]{1,0:T(8,128)(2,1)} copy(bf16[128,512]{1,0:T(8,128)(2,1)} %get-tuple-element.4) | data formatting | bytes 262144
  133.2 1.6 %copy.17 = bf16[128,512]{1,0:T(8,128)(2,1)} copy(bf16[128,512]{1,0:T(8,128)(2,1)} %get-tuple-element.5) | data formatting | bytes 262144

commit v2 on v1

--- a/solution.py
+++ b/solution.py
@@ -26,10 +26,10 @@
 
 def mega_kernel(
     dims,
-    attn, resid, w_out, gain_a, router_t, ids_t, lengths, placement, w_gu, w_d, gain_f,
-    res_out, norm_out,
+    attn, resid, w_out, gain_a, router_t, ids_t, lengths, placement, w_gu, w_d,
+    res_out, scale_out,
     wo, wg, wu, wdo, wdp, p_s, p_r, h1_s, h1_r, f1_s, f1_r, stat_s, stat_r, outb, xs,
-    act_s, act_r, h_s, h_r, f_s, f_r, qx, ret_s, ret_r, fin_s, fin_r, dt, state_ref, wcol,
+    act_s, act_r, h_s, h_r, f_s, f_r, qx, y_s, y_r, ret_s, ret_r, fin_s, fin_r, dt, state_ref, wcol,
     loc, ss, rs,
 ):
     nreq, ny, nt, rows, feat, hid, cap, groups = dims
@@ -38,9 +38,12 @@
     half_rows = rows // 2
     pairs = nreq // 2
     ct = cap // 8
-    per_group = nreq // groups
-    bg = per_group * ct
+    direct = nreq // 2
+    per_group = direct // groups
+    bh = per_group * ct
+    bg = 2 * bh
     grows = bg * 8
+    gh = grows // 2
 
     r = lax.axis_index("req")
     t = lax.axis_index("tp")
@@ -49,6 +52,7 @@
     xr, xl, xo = (x + 1) % nx, (x + nx - 1) % nx, (x + 2) % nx
     tr, tl, to = xr * 2 + c, xl * 2 + c, xo * 2 + c
     tc = x * 2 + (1 - c)
+    sibling = (r // 2) * 2 + (1 - r % 2)
 
     counter = [0]
     started = []
@@ -64,15 +68,17 @@
         started.append(copy)
         return copy
 
-    order = [(dz, dy) for dz in offsets(nz) for dy in offsets(ny)]
-    dest = [((z + dz) % nz) * ny + (y + dy) % ny for dz, dy in order]
-    source = [((z + nz - dz) % nz) * ny + (y + ny - dy) % ny for dz, dy in order]
+    order = [(dz, q) for dz in offsets(nz) for q in range(2)]
+    row_y = (y, ny - 1 - y)
+    dest = [((z + dz) % nz) * ny + row_y[q] for dz, q in order]
+    source = [((z + nz - dz) % nz) * ny + row_y[q] for dz, q in order]
 
     barrier = pltpu.get_barrier_semaphore()
     for k in range(1, nt):
         pl.semaphore_signal(barrier, inc=1, device_id=(r, (t + k) % nt), device_id_type=MESH)
-    for j in range(1, nreq):
+    for j in range(1, direct):
         pl.semaphore_signal(barrier, inc=1, device_id=(dest[j], t), device_id_type=MESH)
+    pl.semaphore_signal(barrier, inc=1, device_id=(sibling, t), device_id_type=MESH)
 
     load_wo = pltpu.make_async_copy(w_out, wo, loc.at[0])
     load_wo.start()
@@ -84,6 +90,45 @@
         )
         for i in range(nx)
     ]
+
+    load_wo.wait()
+    load_wg.start()
+    load_wu.start()
+    for copy in load_wd:
+        copy.start()
+    heads = attn[...]
+    for i in range(nx):
+        w = wo[:, pl.ds(pl.multiple_of((2 * i + 1 - c) * feat, feat), feat)]
+        p_s[i] = jnp.dot(heads, w, preferred_element_type=F32).astype(BF16)
+
+    pl.semaphore_wait(barrier, nt - 1 + direct)
+
+    p_copy = remote(p_s, p_r, r, tc)
+
+    def own_share(i):
+        w = wo[:, pl.ds(pl.multiple_of((2 * i + c) * feat, feat), feat)]
+        return jnp.dot(heads, w, preferred_element_type=F32)
+
+    own = [own_share(i) for i in (xo, xr, xl, x)]
+    p_copy.wait_recv()
+    share = [own[n] + p_r[i].astype(F32) for n, i in enumerate((xo, xr, xl, x))]
+    h1_s[0] = share[0][:half_rows].astype(BF16)
+    h1_s[1] = share[0][half_rows:].astype(BF16)
+    up = remote(h1_s.at[0], h1_r.at[0], r, tr)
+    down = remote(h1_s.at[1], h1_r.at[1], r, tl)
+    low, high = pl.ds(0, half_rows), pl.ds(half_rows, half_rows)
+    f1_s[0, half_rows:] = share[1][half_rows:].astype(BF16)
+    f1_s[1, :half_rows] = share[2][:half_rows].astype(BF16)
+    first = [
+        remote(f1_s.at[0, high], f1_r.at[0, high], r, tr),
+        remote(f1_s.at[1, low], f1_r.at[1, low], r, tl),
+    ]
+    up.wait_recv()
+    f1_s[0, :half_rows] = (share[1][:half_rows] + h1_r[0].astype(F32)).astype(BF16)
+    first.append(remote(f1_s.at[0, low], f1_r.at[0, low], r, tr))
+    down.wait_recv()
+    f1_s[1, half_rows:] = (share[2][half_rows:] + h1_r[1].astype(F32)).astype(BF16)
+    first.append(remote(f1_s.at[1, high], f1_r.at[1, high], r, tl))
 
     e_iota = lax.broadcasted_iota(jnp.int32, (8, rows), 0)
     row_iota = lax.broadcasted_iota(jnp.int32, (8, rows), 1)
@@ -111,54 +156,21 @@
     def column(vec):
         return jnp.transpose(jnp.broadcast_to(vec, (rows, rows)))
 
-    col = lax.broadcasted_iota(jnp.int32, (8, nreq * cap), 1)
-    colkey = jnp.zeros((8, nreq * cap), jnp.int32)
-    for j in range(nreq):
+    col = lax.broadcasted_iota(jnp.int32, (8, direct * cap), 1)
+    colkey = jnp.zeros((8, direct * cap), jnp.int32)
+    for j in range(direct):
         inside = (col >= j * cap) & (col < (j + 1) * cap)
         colkey = jnp.where(inside, (dest[j] // 2) * cap + (col - j * cap), colkey)
     colkey_f = colkey.astype(F32)
     for k in range(2):
         keyc = column(keys[k])
-        for b in range(nreq * cap // 128):
+        for b in range(direct * cap // 128):
             piece = jnp.broadcast_to(colkey_f[0:1, b * 128 : (b + 1) * 128], (rows, 128))
             dt[k, :, b * 128 : (b + 1) * 128] = jnp.where(keyc == piece, 1.0, 0.0).astype(BF16)
 
-    load_wo.wait()
-    load_wg.start()
-    load_wu.start()
-    for copy in load_wd:
-        copy.start()
-    heads = attn[...]
-    for i in range(nx):
-        w = wo[:, pl.ds(pl.multiple_of((2 * i + 1 - c) * feat, feat), feat)]
-        p_s[i] = jnp.dot(heads, w, preferred_element_type=F32).astype(BF16)
-
-    pl.semaphore_wait(barrier, nt - 1 + nreq - 1)
-
-    p_copy = remote(p_s, p_r, r, tc)
-
-    def own_share(i):
-        w = wo[:, pl.ds(pl.multiple_of((2 * i + c) * feat, feat), feat)]
-        return jnp.dot(heads, w, preferred_element_type=F32)
-
-    own = [own_share(i) for i in (xo, xr, xl, x)]
-    p_copy.wait_recv()
-    share = [own[n] + p_r[i].astype(F32) for n, i in enumerate((xo, xr, xl, x))]
-    h1_s[0] = share[0][:half_rows].astype(BF16)
-    h1_s[1] = share[0][half_rows:].astype(BF16)
-    up = remote(h1_s.at[0], h1_r.at[0], r, tr)
-    down = remote(h1_s.at[1], h1_r.at[1], r, tl)
-    up.wait_recv()
-    f1_s[0, :half_rows] = (share[1][:half_rows] + h1_r[0].astype(F32)).astype(BF16)
-    f1_s[0, half_rows:] = share[1][half_rows:].astype(BF16)
-    fup = remote(f1_s.at[0], f1_r.at[0], r, tr)
-    down.wait_recv()
-    f1_s[1, :half_rows] = share[2][:half_rows].astype(BF16)
-    f1_s[1, half_rows:] = (share[2][half_rows:] + h1_r[1].astype(F32)).astype(BF16)
-    fdown = remote(f1_s.at[1], f1_r.at[1], r, tl)
     base = resid[...].astype(F32) + share[3]
-    fup.wait_recv()
-    fdown.wait_recv()
+    for copy in first:
+        copy.wait_recv()
     state = base + f1_r[0].astype(F32) + f1_r[1].astype(F32)
     state_ref[...] = state
 
@@ -175,7 +187,7 @@
 
     stat_s[0:8] = square_sums(state)
     stat_s[8:16] = lax.dot_general(
-        router_t[...] * gain, state, NT, precision=lax.Precision.HIGHEST, preferred_element_type=F32
+        router_t[...].astype(F32) * gain, state, NT, precision=lax.Precision.HIGHEST, preferred_element_type=F32
     )
     stat_copies = [remote(stat_s, stat_r.at[k - 1], r, (t + k) % nt) for k in range(1, nt)]
     total = stat_s[...]
@@ -196,9 +208,11 @@
         outb.at[pl.ds((r // 2) * ct, ct)], xs.at[t, pl.ds(0, ct)], loc.at[3 + nx]
     )
     keep.start()
+    def spot(j):
+        return pl.ds((j // per_group) * bg + (j % per_group) * ct, ct)
+
     a2a = [None] + [
-        remote(outb.at[pl.ds((dest[j] // 2) * ct, ct)], xs.at[t, pl.ds(j * ct, ct)], dest[j], t)
-        for j in range(1, nreq)
+        remote(outb.at[pl.ds((dest[j] // 2) * ct, ct)], xs.at[t, spot(j)], dest[j], t) for j in range(1, direct)
     ]
 
     logits = total[8:16] * inverse
@@ -213,8 +227,14 @@
     reduce = {}
     returns = {}
 
-    def rows_of(g, part=0, parts=1):
-        return pl.ds(g * bg + part * (bg // parts), bg // parts)
+    def rows_of(g):
+        return pl.ds(g * bg, bg)
+
+    def top_of(g):
+        return pl.ds(g * bg, bh)
+
+    def low_of(g):
+        return pl.ds(g * bg + bh, bh)
 
     def stage_a(g):
         for j in range(g * per_group, (g + 1) * per_group):
@@ -222,25 +242,35 @@
                 keep.wait()
             else:
                 a2a[j].wait_recv()
+        mine = xs.at[t, top_of(g)]
+        gather[g, "pair"] = remote(mine, xs.at[t, low_of(g)], sibling, t)
+        gather[g, "top_r"] = remote(mine, mine, r, tr)
+        gather[g, "top_l"] = remote(mine, mine, r, tl)
+
+    def stage_y(g):
+        gather[g, "pair"].wait_recv()
+        mine = xs.at[t, low_of(g)]
+        gather[g, "low_l"] = remote(mine, mine, r, tl)
+        gather[g, "low_r"] = remote(mine, mine, r, tr)
         mine = xs.at[t, rows_of(g)]
-        gather[g, "right"] = remote(mine, mine, r, tr)
-        gather[g, "left"] = remote(mine, mine, r, tl)
         gather[g, "own"] = remote(mine, mine, r, tc)
 
     def stage_b(g):
-        gather[g, "right"].wait_recv()
-        top = xs.at[tl, rows_of(g, 0, 2)]
-        gather[g, "top"] = remote(top, top, r, tr)
-        gather[g, "left"].wait_recv()
-        bottom = xs.at[tr, rows_of(g, 1, 2)]
-        gather[g, "bottom"] = remote(bottom, bottom, r, tl)
+        gather[g, "top_r"].wait_recv()
+        block = xs.at[tl, top_of(g)]
+        gather[g, "top"] = remote(block, block, r, tr)
+        gather[g, "low_l"].wait_recv()
+        block = xs.at[tr, low_of(g)]
+        gather[g, "low"] = remote(block, block, r, tl)
+        gather[g, "top_l"].wait_recv()
+        gather[g, "low_r"].wait_recv()
         for name, who in (("fwd_l", tl), ("fwd_r", tr)):
             block = xs.at[who, rows_of(g)]
             gather[g, name] = remote(block, block, r, tc)
 
     def stage_c(g):
         gather[g, "top"].wait_recv()
-        gather[g, "bottom"].wait_recv()
+        gather[g, "low"].wait_recv()
         block = xs.at[to, rows_of(g)]
         gather[g, "fwd_o"] = remote(block, block, r, tc)
 
@@ -254,9 +284,9 @@
             if name is not None:
                 gather[g, name].wait_recv()
             block = xs[who, g * bg : (g + 1) * bg].reshape(grows, feat)
-            k_rows = pl.ds(pl.multiple_of(who * feat, feat), feat)
-            gp = jnp.dot(block, wg[k_rows, :], preferred_element_type=F32)
-            up_p = jnp.dot(block, wu[k_rows, :], preferred_element_type=F32)
+            k_cols = pl.ds(pl.multiple_of(who * feat, feat), feat)
+            gp = lax.dot_general(block, wg[:, k_cols], NT, preferred_element_type=F32)
+            up_p = lax.dot_general(block, wu[:, k_cols], NT, preferred_element_type=F32)
             gate = gp if gate is None else gate + gp
             up_acc = up_p if up_acc is None else up_acc + up_p
         act_s[g] = (jax.nn.silu(gate) * up_acc).astype(BF16)
@@ -265,8 +295,6 @@
     def product(g, i):
         own_part = jnp.dot(act_s[g], wdo[i], preferred_element_type=F32)
         return own_part + jnp.dot(act_r[g], wdp[i], preferred_element_type=F32)
-
-    gh = grows // 2
 
     def stage_d(g):
         reduce[g, "act"].wait_recv()
@@ -277,29 +305,38 @@
         reduce[g, "down"] = remote(h_s.at[g, 1], h_r.at[g, 1], r, tl)
 
     def stage_e(g):
-        near = product(g, xr)
+        near_r = product(g, xr)
+        f_s[g, 0, gh:] = near_r[gh:].astype(BF16)
+        reduce[g, "r_high"] = remote(f_s.at[g, 0, pl.ds(gh, gh)], f_r.at[g, 0, pl.ds(gh, gh)], r, tr)
+        near_l = product(g, xl)
+        f_s[g, 1, :gh] = near_l[:gh].astype(BF16)
+        reduce[g, "l_low"] = remote(f_s.at[g, 1, pl.ds(0, gh)], f_r.at[g, 1, pl.ds(0, gh)], r, tl)
         reduce[g, "up"].wait_recv()
-        f_s[g, 0, :gh] = (near[:gh] + h_r[g, 0].astype(F32)).astype(BF16)
-        f_s[g, 0, gh:] = near[gh:].astype(BF16)
-        reduce[g, "fup"] = remote(f_s.at[g, 0], f_r.at[g, 0], r, tr)
-        near = product(g, xl)
+        f_s[g, 0, :gh] = (near_r[:gh] + h_r[g, 0].astype(F32)).astype(BF16)
+        reduce[g, "r_low"] = remote(f_s.at[g, 0, pl.ds(0, gh)], f_r.at[g, 0, pl.ds(0, gh)], r, tr)
         reduce[g, "down"].wait_recv()
-        f_s[g, 1, :gh] = near[:gh].astype(BF16)
-        f_s[g, 1, gh:] = (near[gh:] + h_r[g, 1].astype(F32)).astype(BF16)
-        reduce[g, "fdown"] = remote(f_s.at[g, 1], f_r.at[g, 1], r, tl)
+        f_s[g, 1, gh:] = (near_l[gh:] + h_r[g, 1].astype(F32)).astype(BF16)
+        reduce[g, "l_high"] = remote(f_s.at[g, 1, pl.ds(gh, gh)], f_r.at[g, 1, pl.ds(gh, gh)], r, tl)
         qx[g] = product(g, x)
 
     def stage_f(g):
-        reduce[g, "fup"].wait_recv()
-        reduce[g, "fdown"].wait_recv()
-        result = qx[g] + f_r[g, 0].astype(F32) + f_r[g, 1].astype(F32)
-        ret_s[g * bg : (g + 1) * bg] = result.reshape(bg, 8, feat).astype(BF16)
+        for name in ("r_high", "l_low", "r_low", "l_high"):
+            reduce[g, name].wait_recv()
+        low = qx[g, gh:] + f_r[g, 0, gh:].astype(F32) + f_r[g, 1, gh:].astype(F32)
+        y_s[g] = low.astype(BF16)
+        reduce[g, "pair"] = remote(y_s.at[g], y_r.at[g], sibling, t)
+        qx[g, :gh] = qx[g, :gh] + f_r[g, 0, :gh].astype(F32) + f_r[g, 1, :gh].astype(F32)
+
+    def stage_h(g):
+        reduce[g, "pair"].wait_recv()
+        result = qx[g, :gh] + y_r[g].astype(F32)
+        ret_s[g * bh : (g + 1) * bh] = result.reshape(bh, 8, feat).astype(BF16)
         for j in range(g * per_group, (g + 1) * per_group):
+            block = pl.ds(j * ct, ct)
             if j == 0:
-                returns[0] = pltpu.make_async_copy(ret_s.at[pl.ds(0, ct)], ret_r.at[pl.ds(0, ct)], loc.at[4 + nx])
+                returns[0] = pltpu.make_async_copy(ret_s.at[block], ret_r.at[block], loc.at[4 + nx])
                 returns[0].start()
             else:
-                block = pl.ds(j * ct, ct)
                 returns[j] = remote(ret_s.at[block], ret_r.at[block], source[j], t)
 
     def load_down():
@@ -310,36 +347,44 @@
 
     stage_a(0)
     stage_a(1)
+    stage_y(0)
+    stage_y(1)
     stage_b(0)
+    stage_a(2)
+    stage_y(2)
     stage_c(0)
     stage_b(1)
     stage_m(0)
-    stage_a(2)
     load_down()
     stage_d(0)
+    stage_a(3)
+    stage_y(3)
     stage_c(1)
+    stage_b(2)
     stage_m(1)
     stage_e(0)
-    stage_b(2)
-    stage_a(3)
     stage_d(1)
     stage_c(2)
     stage_f(0)
+    stage_b(3)
     stage_m(2)
-    stage_b(3)
     stage_e(1)
     stage_d(2)
+    stage_h(0)
     stage_c(3)
     stage_f(1)
     stage_m(3)
     stage_e(2)
     stage_d(3)
+    stage_h(1)
     stage_e(3)
     stage_f(2)
     stage_f(3)
+    stage_h(2)
+    stage_h(3)
 
     mix = [None, None]
-    half = nreq // 2
+    half = direct // 2
     for part in range(2):
         for j in range(part * half, (part + 1) * half):
             if j == 0:
@@ -353,7 +398,7 @@
             mix[k] = got if mix[k] is None else mix[k] + got
     wide = [jnp.concatenate([wcol[k]] * (feat // rows), axis=1) for k in range(2)]
     combined = state_ref[...] + mix[0] * wide[0] + mix[1] * wide[1]
-    res_out[...] = combined.astype(BF16)
+    res_out[...] = combined
     fin_s[...] = square_sums(combined)
     fin_copies = [remote(fin_s, fin_r.at[k - 1], r, (t + k) % nt) for k in range(1, nt)]
     total = fin_s[...]
@@ -361,8 +406,7 @@
         copy.wait_recv()
         total = total + fin_r[k]
     scale = lax.rsqrt(total[0:1] / full + EPS)
-    scale_col = jnp.concatenate([column(scale)] * (feat // rows), axis=1)
-    norm_out[...] = (combined * scale_col * gain_f[...]).astype(BF16)
+    scale_out[...] = jnp.concatenate([column(scale)] * (feat // rows), axis=1)
     for copy in started:
         copy.wait_send()
     assert counter[0] <= NUM_SEMS, counter[0]
@@ -386,23 +430,25 @@
     ct = cap // 8
     pairs = nreq // 2
     grows = nreq * cap // groups
-    router_t = router.astype(F32).T
+    router_t = router.T
     if experts < 8:
         router_t = jnp.pad(router_t, ((0, 8 - experts), (0, 0)))
     vmem = pl.BlockSpec(memory_space=pltpu.VMEM)
     smem = pl.BlockSpec(memory_space=pltpu.SMEM)
     hbm = pl.BlockSpec(memory_space=pl.ANY)
     dims = (nreq, ny, nt, rows, feat, hid, cap, groups)
-    out = jax.ShapeDtypeStruct((rows, feat), BF16)
-    return pl.pallas_call(
+    combined, scale = pl.pallas_call(
         functools.partial(mega_kernel, dims),
-        out_shape=(out, out),
-        in_specs=[vmem, vmem, hbm, vmem, vmem, vmem, smem, smem, hbm, hbm, vmem],
+        out_shape=(
+            jax.ShapeDtypeStruct((rows, feat), F32),
+            jax.ShapeDtypeStruct((rows, feat), F32),
+        ),
+        in_specs=[vmem, vmem, hbm, vmem, vmem, vmem, smem, smem, hbm, hbm],
         out_specs=(vmem, vmem),
         scratch_shapes=[
             pltpu.VMEM((heads, full), BF16),
-            pltpu.VMEM((full, hid), BF16),
-            pltpu.VMEM((full, hid), BF16),
+            pltpu.VMEM((hid, full), BF16),
+            pltpu.VMEM((hid, full), BF16),
             pltpu.VMEM((nx, hid, feat), BF16),
             pltpu.VMEM((nx, hid, feat), BF16),
             pltpu.VMEM((nx, rows, feat), BF16),
@@ -422,11 +468,13 @@
             pltpu.VMEM((groups, 2, grows, feat), BF16),
             pltpu.VMEM((groups, 2, grows, feat), BF16),
             pltpu.VMEM((groups, grows, feat), F32),
-            pltpu.VMEM((nreq * ct, 8, feat), BF16),
-            pltpu.VMEM((nreq * ct, 8, feat), BF16),
+            pltpu.VMEM((groups, grows // 2, feat), BF16),
+            pltpu.VMEM((groups, grows // 2, feat), BF16),
+            pltpu.VMEM((pairs * ct, 8, feat), BF16),
+            pltpu.VMEM((pairs * ct, 8, feat), BF16),
             pltpu.VMEM((8, rows), F32),
             pltpu.VMEM((nt - 1, 8, rows), F32),
-            pltpu.VMEM((2, rows, nreq * cap), BF16),
+            pltpu.VMEM((2, rows, pairs * cap), BF16),
             pltpu.VMEM((rows, feat), F32),
             pltpu.VMEM((2, rows, rows), F32),
             pltpu.SemaphoreType.DMA((5 + nx,)),
@@ -445,9 +493,12 @@
         expert_ids.T,
         lengths,
         placement,
-        w_gate_up,
+        w_gate_up.transpose(0, 1, 3, 2),
         w_down,
-        gain_final.reshape(1, feat),
+    )
+    return (
+        combined.astype(BF16),
+        (combined * scale * gain_final).astype(BF16),
     )
 
 

time: 135 us -> 119 us (0.88)
  local copies, waits for them, and re-layouts: 14.7 us -> 0.01 us
  Pallas kernels: 118 us -> 116 us
    unnamed x3 -> x2, local copies, waits for them, and re-layouts: 14.7 us -> 0.01 us
    pallas_call x1, Pallas kernels: 118 us -> 116 us  [on_device(): pl.pallas_call(functools.partial(mega_kernel, dims), out_shape=(jax.Shape...]
    convert_element_type x0 -> x1, other arithmetic: none -> 1.87 us  [on_device(): return (combined.astype(BF16), (combined * scale * gain_final).astype(BF16))]
where the time goes in v2:
time: 119 us
  Pallas kernels  116 us (97%)
  other arithmetic  1.87 us (2%)
    pallas_call x1, Pallas kernels, on_device(): pl.pallas_call(functools.partial(mega_kernel, dims), out_shape=(jax.Shape...  116 us

profile of v2, /device:TPU:1, one launch (start us, length us, event | category | flops | bytes accessed | tf_op | source)
XLA Modules:
  0.0 118.8 jit_solution(3434331910806349347)
XLA Ops:
  0.6 0.0 copy-start
  0.6 116.3 %shard_map.122 = (f32[128,512]{1,0:T(8,128)}, f32[128,512]{1,0:T(8,128)}) custom-call(bf16[128,256]{1,0:T(8,128)(2,1)} %attn.1, bf16[128,512]{1,0:T(8,128)(2,1)} %resid.1, bf16[256,4096]{1,0:T(8,128)(2,1)} %w_out.1, f32[1,512]{1,0:T(1,128)} %bitcast.6, bf16[8,512]{1,0:T(8,128)(2,1)} %bitcast.5, s32[2,128]{1,0:T(2,128)} %bitcast.7, s32[1,5]{1,0:T(1,128)} %lengths.1, ...), custom_call_target="tpu_custom_call" | custom-call | tf_op jit(solution)/shard_map/pallas_call | solution.py:440
  116.9 0.0 copy-done
  116.9 1.9 %multiply_convert_fusion = (bf16[128,512]{1,0:T(8,128)(2,1)}, bf16[128,512]{1,0:T(8,128)(2,1)}) fusion(f32[128,512]{1,0:T(8,128)} %get-tuple-element.4, f32[128,512]{1,0:T(8,128)} %get-tuple-element.5, f32[512]{0:T(512)S(1)} %copy-done), kind=kLoop, calls=%fused_computation | loop fusion | flops 262144 | bytes 788480 | tf_op jit(solution)/shard_map/convert_element_type | solution.py:501
Async XLA Ops:
  0.6 116.3 %copy-start = (f32[512]{0:T(512)S(1)}, f32[512]{0:T(512)}, u32[]{:S(2)}) copy-start(f32[512]{0:T(512)} %param.21) | copy-start | bytes 6148
